TPU v7x, 32 devices: a whole 2x2x4 slice. The times are simulated.
32 devices in a mesh: groups: 2 (over y), ep: 4 (over z), half: 2 (over x), tp: 2 (over core).
Axes of the slice: x: 2, y: 2, z: 4, core: 2. Of those that a mesh axis runs over, the one named last changes fastest.
Arguments:
- queries: bfloat16 [512, 2048], P(('groups', 'ep', 'half'), 'tp'), parts along dimension 0, may hold values from -6 to 6
- new_keys: bfloat16 [512, 256], P(('groups', 'ep', 'half'), 'tp'), parts along dimension 0, may hold values from -4 to 4
- new_values: bfloat16 [512, 256], P(('groups', 'ep', 'half'), 'tp'), parts along dimension 0, may hold values from -4 to 4
- cache_keys: bfloat16 [512, 2, 64, 128], P(('groups', 'ep', 'half'), 'tp'), parts along dimension 0, may hold values from -4 to 4
- cache_values: bfloat16 [512, 2, 64, 128], P(('groups', 'ep', 'half'), 'tp'), parts along dimension 0, may hold values from -4 to 4
- lengths: int32 [512], P(('groups', 'ep', 'half')), parts along dimension 0, may hold values from 1 to 64, as said below
- out_weight: bfloat16 [2048, 2048], P('tp', 'half'), may hold values from -0.375 to 0.375
- residual: bfloat16 [512, 2048], P(('groups', 'ep'), 'half'), parts along dimension 0, may hold values from -5 to 5
- norm_gain: float32 [2048], P('half'), may hold values from 0.1 to 1.9
- expert_ids: int32 [512, 8], P(('groups', 'ep')), parts along dimension 0, may hold values from 0 to 63, all different within a row; in each aligned block of 64 rows (0 to 63, 64 to 127, ...) at most 12 rows name the same one
- gate_weights: float32 [512, 8], P(('groups', 'ep')), parts along dimension 0, may hold values from 0.05 to 1
- w_gate: bfloat16 [64, 768, 2048], P(('ep', 'tp'), 'half'), may hold values from -0.125 to 0.125
- w_up: bfloat16 [64, 768, 2048], P(('ep', 'tp'), 'half'), may hold values from -0.125 to 0.125
- w_down: bfloat16 [64, 768, 2048], P(('ep', 'tp'), 'half'), may hold values from -0.625 to 0.625
Outputs:
- layer_out: bfloat16 [512, 2048], P(('groups', 'ep'), ('half', 'tp')), parts along dimension 0
There are 2 independent parts, one for each index of `groups`. A program takes and returns all parts, laid end to end along the dimension named above; an argument that names none is the same for every part. Nothing has to cross between parts.
Inputs may be any that keep to these rules, and one draw needn't show every extreme that they name: `expert_ids`: in each block of 64 consecutive rows (the tokens of one index of ep) no expert is named by more than 12 rows. `lengths`: among each device's 32 requests one has 64 cached tokens.
All inputs are finite; a program needn't handle non-finite values.
Results may differ from a plain program's by a relative error of at most 0.014.
Values may be sent and summed in bfloat16 or wider, within the bound.
No kernel may reach another device: no remote copies, remote signals or barrier semaphores. Data moves between devices by JAX's collectives and lax.ppermute only.
A program may use at most 128 MiB of HBM per device.

v0:
```python
import math
import jax
import jax.numpy as jnp
from jax import lax
from jax.sharding import PartitionSpec as P

EXPERTS = 64
EPSILON = 1e-06


def attend(queries, new_keys, new_values, cache_keys, cache_values, lengths):
    requests, key_heads, context, head_size = cache_keys.shape
    sharing = queries.shape[1] // (key_heads * head_size)
    query_blocks = queries.reshape(requests, key_heads, sharing, head_size)
    score_scale = 1.0 / math.sqrt(head_size)
    scores = (
        jnp.einsum("rkgd,rkcd->rkgc", query_blocks, cache_keys, preferred_element_type=jnp.float32)
        * score_scale
    )
    own_score = (
        jnp.einsum(
            "rkgd,rkd->rkg",
            query_blocks,
            new_keys.reshape(requests, key_heads, head_size),
            preferred_element_type=jnp.float32,
        )
        * score_scale
    )
    valid = lax.iota(jnp.int32, context)[None, :] < lengths[:, None]
    scores = jnp.where(valid[:, None, None, :], scores, -1e30)
    highest = jnp.maximum(jnp.max(scores, axis=-1), own_score)
    weights = jnp.exp(scores - highest[..., None])
    own_weight = jnp.exp(own_score - highest)
    denominator = jnp.sum(weights, axis=-1) + own_weight
    probs = (weights / denominator[..., None]).astype(jnp.bfloat16)
    own_prob = (own_weight / denominator).astype(jnp.bfloat16)
    mixture = jnp.einsum("rkgc,rkcd->rkgd", probs, cache_values, preferred_element_type=jnp.float32)
    mixture = mixture + own_prob.astype(jnp.float32)[..., None] * new_values.reshape(
        requests, key_heads, 1, head_size
    ).astype(jnp.float32)
    return mixture.astype(jnp.bfloat16).reshape(requests, key_heads * sharing * head_size)


def combine_rows(returned_rows, target, gates):
    token_rows, top_count = target.shape
    safe_target = jnp.maximum(target, 0).reshape(-1)
    picked = jnp.take(returned_rows, safe_target, axis=0).reshape(
        token_rows, top_count, returned_rows.shape[1]
    )
    weighting = jnp.where(target >= 0, gates, 0.0)
    return jnp.sum(picked.astype(jnp.float32) * weighting[..., None], axis=1)


def on_device(
    queries,
    new_keys,
    new_values,
    cache_keys,
    cache_values,
    lengths,
    out_weight,
    residual,
    norm_gain,
    expert_ids,
    gate_weights,
    w_gate,
    w_up,
    w_down,
):
    attended = attend(queries, new_keys, new_values, cache_keys, cache_values, lengths)
    partial_mix = jnp.dot(
        lax.all_gather(attended, "half", axis=0, tiled=True),
        out_weight,
        preferred_element_type=jnp.float32,
    )
    mixed = lax.psum(partial_mix.astype(jnp.bfloat16), "tp").astype(jnp.float32)
    hidden = residual.astype(jnp.float32) + mixed
    squares = lax.psum(jnp.sum(hidden * hidden, axis=1), "half")
    half_width = hidden.shape[1]
    width = half_width * lax.axis_size("half")
    normed = (hidden * lax.rsqrt(squares / width + EPSILON)[:, None] * norm_gain[None, :]).astype(
        jnp.bfloat16
    )
    token_rows, top_count = expert_ids.shape
    ep_count = lax.axis_size("ep")
    tp_count = lax.axis_size("tp")
    local_experts = w_gate.shape[0]
    capacity = token_rows * top_count * 3 // (2 * EXPERTS)
    slot_count = ep_count * local_experts * capacity
    flat_ids = expert_ids.reshape(-1)
    one_hot = (flat_ids[:, None] == lax.iota(jnp.int32, EXPERTS)[None, :]).astype(jnp.int32)
    earlier = jnp.cumsum(one_hot, axis=0) - one_hot
    slot = jnp.sum(earlier * one_hot, axis=1)
    owner_ep = flat_ids // (local_experts * tp_count)
    owner_tp = flat_ids // local_experts % tp_count
    target = owner_ep * (local_experts * capacity) + flat_ids % local_experts * capacity + slot
    target = jnp.where(owner_tp == lax.axis_index("tp"), target, -1).reshape(token_rows, top_count)
    dispatch_matrix = jnp.any(
        lax.iota(jnp.int32, slot_count)[:, None, None] == target[None, :, :], axis=2
    ).astype(jnp.bfloat16)
    gates = gate_weights / jnp.sum(gate_weights, axis=1, keepdims=True)
    full_rows = lax.all_gather(normed, "half", axis=1, tiled=True)
    outgoing = jnp.dot(dispatch_matrix, full_rows, preferred_element_type=jnp.float32).astype(
        jnp.bfloat16
    )
    arrived = lax.all_to_all(
        outgoing.reshape(ep_count, local_experts, capacity, width),
        "ep",
        split_axis=0,
        concat_axis=0,
        tiled=True,
    )
    gate_part = jnp.einsum("secd,efd->secf", arrived, w_gate, preferred_element_type=jnp.float32)
    up_part = jnp.einsum("secd,efd->secf", arrived, w_up, preferred_element_type=jnp.float32)
    activation = (jax.nn.silu(gate_part) * up_part).astype(jnp.bfloat16)
    expert_out = jnp.einsum(
        "secf,efd->secd", activation, w_down, preferred_element_type=jnp.float32
    ).astype(jnp.bfloat16)
    summed = lax.psum_scatter(
        expert_out.astype(jnp.float32).astype(jnp.bfloat16), "half", scatter_dimension=3, tiled=True
    ).astype(jnp.float32)
    returned = lax.all_to_all(
        summed.reshape(ep_count, local_experts * capacity, half_width).astype(jnp.bfloat16),
        "ep",
        split_axis=0,
        concat_axis=0,
        tiled=True,
    ).astype(jnp.float32)
    term = combine_rows(returned.reshape(slot_count, half_width), target, gates)
    expert_sum = lax.psum_scatter(
        term.astype(jnp.bfloat16), "tp", scatter_dimension=1, tiled=True
    ).astype(jnp.float32)
    slice_width = expert_sum.shape[1]
    own_columns = lax.dynamic_slice_in_dim(
        hidden, lax.axis_index("tp") * slice_width, slice_width, 1
    )
    return (own_columns + expert_sum).astype(jnp.bfloat16)


def solution(mesh):
    placed = (
        P(("groups", "ep", "half"), "tp"),
        P(("groups", "ep", "half"), "tp"),
        P(("groups", "ep", "half"), "tp"),
        P(("groups", "ep", "half"), "tp", None, None),
        P(("groups", "ep", "half"), "tp", None, None),
        P(("groups", "ep", "half")),
        P("tp", "half"),
        P(("groups", "ep"), "half"),
        P("half"),
        P(("groups", "ep"), None),
        P(("groups", "ep"), None),
        P(("ep", "tp"), "half", None),
        P(("ep", "tp"), "half", None),
        P(("ep", "tp"), "half", None),
    )
    return jax.shard_map(
        on_device,
        mesh=mesh,
        in_specs=placed,
        out_specs=P(("groups", "ep"), ("half", "tp")),
        check_vma=False,
    )
```

profile of v0, /device:TPU:0, one launch (start us, length us, event | category | flops | bytes accessed | tf_op | source)
XLA Modules:
  0.0 210.5 jit_solution(17106588360139845303)
XLA Ops:
  6.5 1.0 copy.78
  7.5 0.7 iota_compare_fusion.3
  8.3 0.8 fusion.58
  9.1 1.5 fusion.76
  10.9 0.7 convert_element_type.73
  11.6 1.4 fusion.41
  13.0 6.0 %all_gather.6 = bf16[64,1024]{1,0:T(8,128)(2,1)S(1)} all-gather(bf16[32,1024]{1,0:T(8,128)(2,1)S(1)} %bitcast.97), channel_id=1, replica_groups=mesh['groups'=2,'ep'=4,'half'=2,'tp'=2] {'half'}, dimensions={0}, use_global_device_ids=true | all-gather | bytes 196608 | tf_op jit(solution)/shard_map/all_gather | solution.py:72
  19.0 1.1 convolution_convert_fusion.1
  20.5 1.2 reduce-window.6
  22.4 0.3 fusion.47
  22.7 17.3 %all-reduce.2.cloned.1.call-done = bf16[64,1024]{1,0:T(8,128)(2,1)} async-done(((bf16[64,1024]{1,0:T(8,128)(2,1)}), bf16[64,1024]{1,0:T(8,128)(2,1)}) %all-reduce.2.cloned.1.call-update) | async-done | bytes 131088 | tf_op jit(solution)/shard_map/psum | solution.py:76
  40.0 1.0 convert_add_fusion
  41.0 4.9 %psum.15 = f32[64]{0:T(128)S(1)} all-reduce(f32[64]{0:T(128)S(1)} %get-tuple-element.8), channel_id=1, replica_groups=mesh['groups'=2,'ep'=4,'half'=2,'tp'=2] {'half'}, use_global_device_ids=true, to_apply=%region_8.9 | all-reduce | flops 64 | bytes 512 | tf_op jit(solution)/shard_map/psum | solution.py:78
  46.0 1.0 multiply_convert_fusion
  47.0 5.6 %all_gather.7 = bf16[64,2048]{1,0:T(8,128)(2,1)S(1)} all-gather(bf16[64,1024]{1,0:T(8,128)(2,1)S(1)} %multiply_convert_fusion), channel_id=1, replica_groups=mesh['groups'=2,'ep'=4,'half'=2,'tp'=2] {'half'}, dimensions={1}, use_global_device_ids=true | all-gather | bytes 393216 | tf_op jit(solution)/shard_map/all_gather | solution.py:102
  52.6 1.8 convolution_convert_fusion
  54.4 3.6 %reshape.224 = bf16[4,8,12,2048]{3,2,1,0:T(8,128)(2,1)} reshape(bf16[384,2048]{1,0:T(8,128)(2,1)} %convolution_convert_fusion) | data formatting | bytes 3145728 | tf_op jit(solution)/shard_map/reshape | solution.py:107
  58.0 2.5 %copy.65 = bf16[4,8,12,2048]{3,1,2,0:T(8,128)(2,1)S(1)} copy(bf16[4,8,12,2048]{3,2,1,0:T(8,128)(2,1)} %reshape.224) | data formatting | bytes 3145728 | tf_op jit(solution)/shard_map/reshape | solution.py:107
  60.5 39.8 %all_to_all.10 = bf16[4,8,12,2048]{3,1,2,0:T(8,128)(2,1)S(1)} all-to-all(bf16[4,8,12,2048]{3,1,2,0:T(8,128)(2,1)S(1)} %copy.65), channel_id=1, replica_groups=mesh['groups'=2,'ep'=4,'half'=2,'tp'=2] {'ep'}, dimensions={0} | all-to-all | bytes 3145728 | tf_op jit(solution)/shard_map/all_to_all | solution.py:106
  100.2 1.1 copy-done.1
  101.4 8.7 %fusion.16 = f32[4,8,12,384]{3,2,0,1:T(8,128)S(1)} fusion(bf16[8,384,2048]{2,1,0:T(8,128)(2,1)} %param.25, bf16[4,8,12,2048]{3,1,2,0:T(8,128)(2,1)S(1)} %all_to_all.10), kind=kOutput, calls=%fused_computation.15 | convolution fusion | flops 603979776 | bytes 14745600 | tf_op jit(solution)/shard_map/secd,efd->secf/dot_general | solution.py:113
  110.1 18.4 %fusion.9 = bf16[4,8,12,2048]{3,2,0,1:T(8,128)(2,1)} fusion(bf16[8,384,2048]{2,1,0:T(8,128)(2,1)} %param.27, bf16[8,384,2048]{2,1,0:T(8,128)(2,1)} %param.26, bf16[4,8,12,2048]{3,1,2,0:T(8,128)(2,1)} %copy-done.1, f32[4,8,12,384]{3,2,0,1:T(8,128)S(1)} %fusion.16), kind=kOutput, calls=%fused_computation.9 | convolution fusion | flops 1209630720 | bytes 28901376 | tf_op jit(solution)/shard_map/secf,efd->secd/dot_general | solution.py:116
  128.5 31.1 %reduce-scatter.3.cloned.1.call-done = bf16[4,8,12,1024]{3,2,0,1:T(8,128)(2,1)} async-done(((bf16[4,8,12,2048]{3,2,0,1:T(8,128)(2,1)}), bf16[4,8,12,1024]{3,2,0,1:T(8,128)(2,1)}) %reduce-scatter.3.cloned.1.call-update) | async-done | bytes 786448 | tf_op jit(solution)/shard_map/reduce_scatter | solution.py:119
  159.6 1.8 copy.68
  161.4 1.1 copy.69
  162.5 4.6 %all-to-all-start.1 = ((bf16[4,96,1024]{2,1,0:T(8,128)(2,1)}), bf16[4,96,1024]{2,1,0:T(8,128)(2,1)S(1)}, u32[]{:S(2)}, u32[]{:S(2)}) async-start(bf16[4,96,1024]{2,1,0:T(8,128)(2,1)} %copy.69), calls=%async_computation.2 | async-start | bytes 1572864 | tf_op jit(solution)/shard_map/all_to_all | solution.py:122
  167.6 19.5 %all-to-all-done.1 = bf16[4,96,1024]{2,1,0:T(8,128)(2,1)S(1)} async-done(((bf16[4,96,1024]{2,1,0:T(8,128)(2,1)}), bf16[4,96,1024]{2,1,0:T(8,128)(2,1)S(1)}, u32[]{:S(2)}, u32[]{:S(2)}) %all-to-all-start.1) | async-done | bytes 786464 | tf_op jit(solution)/shard_map/all_to_all | solution.py:122
  187.1 1.4 bitcast_convert_fusion
  188.5 5.1 %gather_fusion = f32[512,1024]{1,0:T(8,128)} fusion(f32[384,1024]{1,0:T(8,128)} %bitcast_convert_fusion, s32[1024]{0:T(1024)S(1)} %pad_clamp_fusion), kind=kCustom, calls=%fused_computation | custom fusion | bytes 4196352 | tf_op jit(solution)/shard_map/jit(_take)/gather | solution.py:47
  193.5 3.0 %fusion.15 = bf16[64,1024]{1,0:T(8,128)(2,1)} fusion(f32[512,1024]{1,0:T(8,128)} %gather_fusion, f32[64,8]{1,0:T(8,128)S(1)} %copy.71, pred[64,8]{1,0:T(8,128)(4,1)S(1)} %copy.63), kind=kLoop, calls=%fused_computation.14 | loop fusion | flops 1507328 | bytes 2230784 | tf_op jit(solution)/shard_map/reduce_sum | solution.py:51
  196.6 5.9 %reduce-scatter.5.cloned.1.call-done = bf16[64,512]{1,0:T(8,128)(2,1)} async-done(((bf16[64,1024]{1,0:T(8,128)(2,1)}), bf16[64,512]{1,0:T(8,128)(2,1)}) %reduce-scatter.5.cloned.1.call-update) | async-done | bytes 65552 | tf_op jit(solution)/shard_map/reduce_scatter | solution.py:130
  202.5 1.5 add_convert_fusion
  (43 shorter events, 1.7 us)
Async XLA Ops:
  6.5 12.4 %copy-start = (bf16[1024,1024]{1,0:T(8,128)(2,1)S(1)}, bf16[1024,1024]{1,0:T(8,128)(2,1)}, u32[]{:S(2)}) copy-start(bf16[1024,1024]{1,0:T(8,128)(2,1)} %param.20) | copy-start | bytes 6291460
  6.5 33.5 %all-reduce.2.cloned.1.call-start = ((), (), s32[]{:S(2)}) async-start(), calls=%async_computation.4 | async-start | bytes 262144 | tf_op jit(solution)/shard_map/psum | solution.py:76
  10.6 9.5 %copy-start.3 = (s32[64,8]{0,1:T(8,128)S(1)}, s32[64,8]{0,1:T(8,128)}, u32[]{:S(2)}) copy-start(s32[64,8]{0,1:T(8,128)} %param.23) | copy-start | bytes 6148
  12.9 27.1 %copy-start.2 = (bf16[64,1024]{1,0:T(8,128)(2,1)S(1)}, bf16[64,1024]{1,0:T(8,128)(2,1)}, u32[]{:S(2)}) copy-start(bf16[64,1024]{1,0:T(8,128)(2,1)} %param.21) | copy-start | bytes 393220
  13.0 33.0 %copy-start.5 = (f32[1024]{0:T(1024)S(1)}, f32[1024]{0:T(1024)}, u32[]{:S(2)}) copy-start(f32[1024]{0:T(1024)} %param.22) | copy-start | bytes 12292
  20.1 139.5 %reduce-scatter.3.cloned.1.call-start = ((), (), s32[]{:S(2)}) async-start(), calls=%async_computation.5 | async-start | bytes 3145728 | tf_op jit(solution)/shard_map/reduce_scatter | solution.py:119
  100.2 1.1 copy-start.1
  128.5 38.8 %copy-start.4 = (f32[64,8]{0,1:T(8,128)S(1)}, f32[64,8]{0,1:T(8,128)}, u32[]{:S(2)}) copy-start(f32[64,8]{0,1:T(8,128)} %param.24) | copy-start | bytes 6148
  162.5 24.5 %all-to-all-start.1 = ((bf16[4,96,1024]{2,1,0:T(8,128)(2,1)}), bf16[4,96,1024]{2,1,0:T(8,128)(2,1)S(1)}, u32[]{:S(2)}, u32[]{:S(2)}) async-start(bf16[4,96,1024]{2,1,0:T(8,128)(2,1)} %copy.69), calls=%async_computation.2 | async-start | bytes 1572864 | tf_op jit(solution)/shard_map/all_to_all | solution.py:122
  167.1 35.3 %reduce-scatter.5.cloned.1.call-start = ((), (), s32[]{:S(2)}) async-start(), calls=%async_computation.6 | async-start | bytes 196608 | tf_op jit(solution)/shard_map/reduce_scatter | solution.py:130
Sparse Core Ops, SparseCore 0:
  20.2 19.6 all-reduce.1
  128.6 30.9 reduce-scatter.2
  196.7 5.7 reduce-scatter.4
where the time goes:
time: 211 us; the launch traced here: 210 us
  waiting for transfers between devices  73.9 us (35%)
  blocking collectives  56.3 us (27%)
  matrix products  33.7 us (16%)
  local copies, waits for them, and re-layouts  17.4 us (8%)
  between operations  13.3 us (6%)
  other arithmetic  11.3 us (5%)
  starting transfers between devices  4.62 us (2%)
    all_to_all x1, blocking collectives, on_device(): lax.all_to_all(outgoing.reshape(ep_count, local_experts, capacity, width)...  39.8 us
    reduce_scatter x1, waiting for transfers between devices, on_device(): lax.psum_scatter(expert_out.astype(jnp.float32).astype(jnp.bfloat16), 'ha...  31.1 us
    all_to_all x1, waiting for transfers between devices, on_device(): lax.all_to_all(summed.reshape(ep_count, local_experts * capacity, half_wi...  19.5 us
    dot_general x1, matrix products, on_device(): jnp.einsum('secf,efd->secd', activation, w_down, preferred_element_type=j...  18.4 us
    psum x1, waiting for transfers between devices, on_device(): mixed = lax.psum(partial_mix.astype(jnp.bfloat16), 'tp').astype(jnp.float32)  17.3 us
    dot_general x1, matrix products, on_device(): jnp.einsum('secd,efd->secf', arrived, w_gate, preferred_element_type=jnp....  8.68 us
    reshape x2, local copies, waits for them, and re-layouts, on_device(): outgoing.reshape(ep_count, local_experts, capacity, width)  6.06 us
    all_gather x1, blocking collectives, on_device(): lax.all_gather(attended, 'half', axis=0, tiled=True)  6 us
  transfers between devices with their start and end apart: 4, of which 4 were waited for; matrix products, arithmetic and copies ran while one was open for 1% of the time, Pallas kernels for 0%

commit v1 on v0

--- a/solution.py
+++ b/solution.py
@@ -6,6 +6,11 @@
 
 EXPERTS = 64
 EPSILON = 1e-06
+
+
+def gather_and_add(x, axis):
+    parts = lax.all_gather(x, axis)
+    return jnp.sum(parts, axis=0)
 
 
 def attend(queries, new_keys, new_values, cache_keys, cache_values, lengths):
@@ -73,7 +78,7 @@
         out_weight,
         preferred_element_type=jnp.float32,
     )
-    mixed = lax.psum(partial_mix.astype(jnp.bfloat16), "tp").astype(jnp.float32)
+    mixed = gather_and_add(partial_mix.astype(jnp.bfloat16), "tp").astype(jnp.float32)
     hidden = residual.astype(jnp.float32) + mixed
     squares = lax.psum(jnp.sum(hidden * hidden, axis=1), "half")
     half_width = hidden.shape[1]

time: 211 us -> 195 us (0.924)
  waiting for transfers between devices: 73.9 us -> 56.6 us
  blocking collectives: 56.3 us -> 58.6 us
    psum x1 -> x0, waiting for transfers between devices: 17.3 us -> none  [on_device(): mixed = lax.psum(partial_mix.astype(jnp.bfloat16), 'tp').astype(jnp.float32)]
  transfers between devices with their start and end apart: 4 -> 3, of which waited for: 4 -> 3; matrix products, arithmetic and copies ran while one was open for 1% -> 0% of each run, Pallas kernels for 0% -> 0%
where the time goes in v1:
time: 195 us; the launch traced here: 194 us
  blocking collectives  58.6 us (30%)
  waiting for transfers between devices  56.6 us (29%)
  matrix products  33 us (17%)
  local copies, waits for them, and re-layouts  18 us (9%)
  between operations  13.6 us (7%)
  other arithmetic  9.58 us (5%)
  starting transfers between devices  4.59 us (2%)
    all_to_all x1, blocking collectives, on_device(): lax.all_to_all(outgoing.reshape(ep_count, local_experts, capacity, width)...  40.2 us
    reduce_scatter x1, waiting for transfers between devices, on_device(): lax.psum_scatter(expert_out.astype(jnp.float32).astype(jnp.bfloat16), 'ha...  31.2 us
    all_to_all x1, waiting for transfers between devices, on_device(): lax.all_to_all(summed.reshape(ep_count, local_experts * capacity, half_wi...  19.5 us
    dot_general x1, matrix products, on_device(): jnp.einsum('secf,efd->secd', activation, w_down, preferred_element_type=j...  18.4 us
    dot_general x1, matrix products, on_device(): jnp.einsum('secd,efd->secf', arrived, w_gate, preferred_element_type=jnp....  8.69 us
    reshape x2, local copies, waits for them, and re-layouts, on_device(): outgoing.reshape(ep_count, local_experts, capacity, width)  6.06 us
    reduce_scatter x1, waiting for transfers between devices, on_device(): lax.psum_scatter(term.astype(jnp.bfloat16), 'tp', scatter_dimension=1, ti...  5.87 us
    all_gather x1, blocking collectives, on_device(): lax.all_gather(attended, 'half', axis=0, tiled=True)  5.86 us
  transfers between devices with their start and end apart: 3, of which 3 were waited for; matrix products, arithmetic and copies ran while one was open for 0% of the time, Pallas kernels for 0%

profile of v1, /device:TPU:0, one launch (start us, length us, event | category | flops | bytes accessed | tf_op | source)
XLA Modules:
  0.0 194.1 jit_solution(10395389772654285416)
XLA Ops:
  6.5 0.9 copy.59
  7.6 0.9 copy.78
  8.5 0.7 iota_compare_fusion.3
  9.2 0.8 fusion.58
  10.1 1.5 fusion.76
  11.8 0.7 convert_element_type.75
  12.5 1.4 fusion.41
  13.9 5.9 %all_gather.12 = bf16[64,1024]{1,0:T(8,128)(2,1)S(1)} all-gather(bf16[32,1024]{1,0:T(8,128)(2,1)S(1)} %bitcast.99), channel_id=1, replica_groups=mesh['groups'=2,'ep'=4,'half'=2,'tp'=2] {'half'}, dimensions={0}, use_global_device_ids=true | all-gather | bytes 196608 | tf_op jit(solution)/shard_map/all_gather | solution.py:77
  19.8 0.5 convolution_convert_fusion.1
  20.3 2.0 %all-gather = bf16[128,1024]{1,0:T(8,128)(2,1)S(1)} all-gather(bf16[64,1024]{1,0:T(8,128)(2,1)S(1)} %convolution_convert_fusion.1), channel_id=2, replica_groups=mesh['groups'=2,'ep'=4,'half'=2,'tp'=2] {'tp'}, dimensions={0}, use_global_device_ids=true | all-gather | bytes 393216 | tf_op jit(solution)/shard_map/all_gather | solution.py:12
  22.5 4.9 %psum.7 = f32[64]{0:T(128)S(1)} all-reduce(f32[64]{0:T(128)S(1)} %get-tuple-element.8), channel_id=1, replica_groups=mesh['groups'=2,'ep'=4,'half'=2,'tp'=2] {'half'}, use_global_device_ids=true, to_apply=%region_8.9 | all-reduce | flops 64 | bytes 512 | tf_op jit(solution)/shard_map/psum | solution.py:83
  27.6 5.6 %all_gather.15 = bf16[64,2048]{1,0:T(8,128)(2,1)S(1)} all-gather(bf16[64,1024]{1,0:T(8,128)(2,1)S(1)} %multiply_convert_fusion), channel_id=1, replica_groups=mesh['groups'=2,'ep'=4,'half'=2,'tp'=2] {'half'}, dimensions={1}, use_global_device_ids=true | all-gather | bytes 393216 | tf_op jit(solution)/shard_map/all_gather | solution.py:107
  33.2 1.2 reduce-window.6
  34.4 0.2 slice_reduce_fusion
  35.1 0.3 fusion.47
  35.4 1.8 convolution_convert_fusion
  37.2 3.6 %reshape.224 = bf16[4,8,12,2048]{3,2,1,0:T(8,128)(2,1)} reshape(bf16[384,2048]{1,0:T(8,128)(2,1)} %convolution_convert_fusion) | data formatting | bytes 3145728 | tf_op jit(solution)/shard_map/reshape | solution.py:112
  40.8 2.5 %copy.65 = bf16[4,8,12,2048]{3,1,2,0:T(8,128)(2,1)S(1)} copy(bf16[4,8,12,2048]{3,2,1,0:T(8,128)(2,1)} %reshape.224) | data formatting | bytes 3145728 | tf_op jit(solution)/shard_map/reshape | solution.py:112
  43.2 40.2 %all_to_all.10 = bf16[4,8,12,2048]{3,1,2,0:T(8,128)(2,1)S(1)} all-to-all(bf16[4,8,12,2048]{3,1,2,0:T(8,128)(2,1)S(1)} %copy.65), channel_id=1, replica_groups=mesh['groups'=2,'ep'=4,'half'=2,'tp'=2] {'ep'}, dimensions={0} | all-to-all | bytes 3145728 | tf_op jit(solution)/shard_map/all_to_all | solution.py:111
  83.4 1.1 copy-done.1
  84.6 8.7 %fusion.16 = f32[4,8,12,384]{3,2,0,1:T(8,128)S(1)} fusion(bf16[8,384,2048]{2,1,0:T(8,128)(2,1)} %param.25, bf16[4,8,12,2048]{3,1,2,0:T(8,128)(2,1)S(1)} %all_to_all.10), kind=kOutput, calls=%fused_computation.15 | convolution fusion | flops 603979776 | bytes 14745600 | tf_op jit(solution)/shard_map/secd,efd->secf/dot_general | solution.py:118
  93.3 18.4 %fusion.9 = bf16[4,8,12,2048]{3,2,0,1:T(8,128)(2,1)} fusion(bf16[8,384,2048]{2,1,0:T(8,128)(2,1)} %param.27, bf16[8,384,2048]{2,1,0:T(8,128)(2,1)} %param.26, bf16[4,8,12,2048]{3,1,2,0:T(8,128)(2,1)} %copy-done.1, f32[4,8,12,384]{3,2,0,1:T(8,128)S(1)} %fusion.16), kind=kOutput, calls=%fused_computation.9 | convolution fusion | flops 1209630720 | bytes 28901376 | tf_op jit(solution)/shard_map/secf,efd->secd/dot_general | solution.py:121
  111.7 31.2 %reduce-scatter.3.cloned.1.call-done = bf16[4,8,12,1024]{3,2,0,1:T(8,128)(2,1)} async-done(((bf16[4,8,12,2048]{3,2,0,1:T(8,128)(2,1)}), bf16[4,8,12,1024]{3,2,0,1:T(8,128)(2,1)}) %reduce-scatter.3.cloned.1.call-update) | async-done | bytes 786448 | tf_op jit(solution)/shard_map/reduce_scatter | solution.py:124
  142.9 1.8 copy.68
  144.7 1.1 copy.69
  145.8 4.6 %all-to-all-start.1 = ((bf16[4,96,1024]{2,1,0:T(8,128)(2,1)}), bf16[4,96,1024]{2,1,0:T(8,128)(2,1)S(1)}, u32[]{:S(2)}, u32[]{:S(2)}) async-start(bf16[4,96,1024]{2,1,0:T(8,128)(2,1)} %copy.69), calls=%async_computation.2 | async-start | bytes 1572864 | tf_op jit(solution)/shard_map/all_to_all | solution.py:127
  150.9 19.5 %all-to-all-done.1 = bf16[4,96,1024]{2,1,0:T(8,128)(2,1)S(1)} async-done(((bf16[4,96,1024]{2,1,0:T(8,128)(2,1)}), bf16[4,96,1024]{2,1,0:T(8,128)(2,1)S(1)}, u32[]{:S(2)}, u32[]{:S(2)}) %all-to-all-start.1) | async-done | bytes 786464 | tf_op jit(solution)/shard_map/all_to_all | solution.py:127
  170.4 1.4 bitcast_convert_fusion
  171.7 5.1 %gather_fusion = f32[512,1024]{1,0:T(8,128)} fusion(f32[384,1024]{1,0:T(8,128)} %bitcast_convert_fusion, s32[1024]{0:T(1024)S(1)} %pad_clamp_fusion), kind=kCustom, calls=%fused_computation | custom fusion | bytes 4196352 | tf_op jit(solution)/shard_map/jit(_take)/gather | solution.py:52
  176.8 3.0 %fusion.15 = bf16[64,1024]{1,0:T(8,128)(2,1)} fusion(f32[512,1024]{1,0:T(8,128)} %gather_fusion, f32[64,8]{1,0:T(8,128)S(1)} %copy.71, pred[64,8]{1,0:T(8,128)(4,1)S(1)} %copy.63), kind=kLoop, calls=%fused_computation.14 | loop fusion | flops 1507328 | bytes 2230784 | tf_op jit(solution)/shard_map/reduce_sum | solution.py:56
  179.9 5.9 %reduce-scatter.5.cloned.1.call-done = bf16[64,512]{1,0:T(8,128)(2,1)} async-done(((bf16[64,1024]{1,0:T(8,128)(2,1)}), bf16[64,512]{1,0:T(8,128)(2,1)}) %reduce-scatter.5.cloned.1.call-update) | async-done | bytes 65552 | tf_op jit(solution)/shard_map/reduce_scatter | solution.py:135
  185.7 1.5 add_convert_fusion
  (42 shorter events, 1.6 us)
Async XLA Ops:
  6.5 13.3 %copy-start = (bf16[1024,1024]{1,0:T(8,128)(2,1)S(1)}, bf16[1024,1024]{1,0:T(8,128)(2,1)}, u32[]{:S(2)}) copy-start(bf16[1024,1024]{1,0:T(8,128)(2,1)} %param.20) | copy-start | bytes 6291460
  6.5 136.3 %reduce-scatter.3.cloned.1.call-start = ((), (), s32[]{:S(2)}) async-start(), calls=%async_computation.4 | async-start | bytes 3145728 | tf_op jit(solution)/shard_map/reduce_scatter | solution.py:124
  12.5 9.8 %copy-start.2 = (bf16[64,1024]{1,0:T(8,128)(2,1)S(1)}, bf16[64,1024]{1,0:T(8,128)(2,1)}, u32[]{:S(2)}) copy-start(bf16[64,1024]{1,0:T(8,128)(2,1)} %param.21) | copy-start | bytes 393220
  13.9 13.5 %copy-start.5 = (f32[1024]{0:T(1024)S(1)}, f32[1024]{0:T(1024)}, u32[]{:S(2)}) copy-start(f32[1024]{0:T(1024)} %param.22) | copy-start | bytes 12292
  19.8 15.2 %copy-start.3 = (s32[64,8]{0,1:T(8,128)S(1)}, s32[64,8]{0,1:T(8,128)}, u32[]{:S(2)}) copy-start(s32[64,8]{0,1:T(8,128)} %param.23) | copy-start | bytes 6148
  83.4 1.1 copy-start.1
  111.6 39.0 %copy-start.4 = (f32[64,8]{0,1:T(8,128)S(1)}, f32[64,8]{0,1:T(8,128)}, u32[]{:S(2)}) copy-start(f32[64,8]{0,1:T(8,128)} %param.24) | copy-start | bytes 6148
  145.8 24.5 %all-to-all-start.1 = ((bf16[4,96,1024]{2,1,0:T(8,128)(2,1)}), bf16[4,96,1024]{2,1,0:T(8,128)(2,1)S(1)}, u32[]{:S(2)}, u32[]{:S(2)}) async-start(bf16[4,96,1024]{2,1,0:T(8,128)(2,1)} %copy.69), calls=%async_computation.2 | async-start | bytes 1572864 | tf_op jit(solution)/shard_map/all_to_all | solution.py:127
  150.4 35.3 %reduce-scatter.5.cloned.1.call-start = ((), (), s32[]{:S(2)}) async-start(), calls=%async_computation.5 | async-start | bytes 196608 | tf_op jit(solution)/shard_map/reduce_scatter | solution.py:135
Sparse Core Ops, SparseCore 0:
  111.8 31.0 reduce-scatter.2
  180.0 5.7 reduce-scatter.4
